TPU v7x, 32 devices: a whole 2x2x4 slice. The times are simulated.
32 devices in a mesh: expert: 8 (over z, y), dp: 4 (over x, core).
Axes of the slice: x: 2, y: 2, z: 4, core: 2. Of those that a mesh axis runs over, the one named last changes fastest.
Arguments:
- grad_parts: bfloat16 [4, 8, 3584, 1024], P('dp', 'expert'), may hold values from -6 to 6
- owner_slot: int32 [8], replicated, may hold values from 0 to 7, each once
- slot_expert: int32 [8, 2], replicated, may hold values from 0 to 7, all different within a row
- master: float32 [8, 3584, 1024], P(None, 'expert', 'dp'), may hold values from -1.5 to 1.5
- moment_one: float32 [8, 3584, 1024], P(None, 'expert', 'dp'), may hold values from -2 to 2
- moment_two: float32 [8, 3584, 1024], P(None, 'expert', 'dp'), may hold values from 0.01 to 1
- ema_weights: float32 [8, 3584, 1024], P(None, 'expert', 'dp'), may hold values from -1.5 to 1.5
Outputs:
- master_out: float32 [8, 3584, 1024], P(None, 'expert', 'dp')
- moment_one_out: float32 [8, 3584, 1024], P(None, 'expert', 'dp')
- moment_two_out: float32 [8, 3584, 1024], P(None, 'expert', 'dp')
- ema_out: float32 [8, 3584, 1024], P(None, 'expert', 'dp')
- replicas: bfloat16 [16, 3584, 1024], P('expert', None, 'dp')
Inputs may be any that keep to these rules, and one draw needn't show every extreme that they name: `owner_slot`: a permutation of the 8 experts; position k belongs to expert-axis index k. `slot_expert`: each row names 2 different experts, and every expert is named by some row.
All inputs are finite; a program needn't handle non-finite values.
Results may differ from a plain program's by a relative error of at most 0.009.
Values may be sent and summed in bfloat16 or wider, within the bound.
A program may use at most 128 MiB of HBM per device.

v0:
```python
import jax
import jax.numpy as jnp
from jax import lax
from jax.sharding import PartitionSpec as P

STEP = 10


beta_one = 0.9
beta_two = 0.999
adam_eps = 1e-08
learn_rate = 0.05
decay_rate = 0.1
ema_decay = 0.99


def per_device(grad_parts, owner_slot, slot_expert, master, moment_one, moment_two, ema_weights):
    summed = lax.psum_scatter(
        grad_parts[0].astype(jnp.float32).astype(jnp.bfloat16),
        "dp",
        scatter_dimension=2,
        tiled=True,
    ).astype(jnp.float32)
    owner_rows = lax.all_to_all(
        summed.astype(jnp.bfloat16), "expert", split_axis=1, concat_axis=0, tiled=True
    ).astype(summed.dtype)
    gradient = jnp.take(owner_rows, owner_slot, axis=0)
    correct_one = 1.0 - beta_one**STEP
    correct_two = 1.0 - beta_two**STEP
    moment_one_out = beta_one * moment_one + (1.0 - beta_one) * gradient
    moment_two_out = beta_two * moment_two + (1.0 - beta_two) * gradient * gradient
    update = moment_one_out / correct_one / (jnp.sqrt(moment_two_out / correct_two) + adam_eps)
    master_out = master - learn_rate * (update + decay_rate * master)
    ema_out = ema_decay * ema_weights + (1.0 - ema_decay) * master_out
    updated_bf16 = master_out.astype(jnp.bfloat16)
    outgoing = jnp.take(updated_bf16, slot_expert.reshape(-1), axis=0)
    replicas = lax.all_to_all(outgoing, "expert", split_axis=0, concat_axis=1, tiled=True)
    return (master_out, moment_one_out, moment_two_out, ema_out, replicas)


def solution(mesh):
    placed = (
        P("dp", "expert", None, None),
        P(),
        P(),
        P(None, "expert", "dp"),
        P(None, "expert", "dp"),
        P(None, "expert", "dp"),
        P(None, "expert", "dp"),
    )
    return jax.shard_map(
        per_device,
        mesh=mesh,
        in_specs=placed,
        out_specs=(
            P(None, "expert", "dp"),
            P(None, "expert", "dp"),
            P(None, "expert", "dp"),
            P(None, "expert", "dp"),
            P("expert", None, "dp"),
        ),
        check_vma=False,
    )
```

profile of v0, /device:TPU:0, one launch (start us, length us, event | category | flops | bytes accessed | tf_op | source)
XLA Modules:
  0.0 281.6 jit_solution(11911839623130922514)
XLA Ops:
  7.2 0.0 reduce-scatter.2.cloned.1.call-start
  7.2 0.7 reduce-scatter.2.cloned.1.call-update
  7.9 69.9 %reduce-scatter.2.cloned.1.call-done = bf16[1,3584,256]{2,1,0:T(8,128)(2,1)} async-done(((bf16[1,3584,1024]{2,1,0:T(8,128)(2,1)}), bf16[1,3584,256]{2,1,0:T(8,128)(2,1)}) %reduce-scatter.2.cloned.1.call-update) | async-done | bytes 1835024 | tf_op jit(solution)/shard_map/reduce_scatter | solution.py:18
  77.8 6.8 %copy.27 = bf16[1,3584,256]{2,0,1:T(2,128)(2,1)} copy(bf16[1,3584,256]{2,1,0:T(8,128)(2,1)} %reduce-scatter.2.cloned.1.call-done) | data formatting | bytes 3670016 | tf_op jit(solution)/shard_map/reduce_scatter | solution.py:18
  84.6 0.5 broadcast.61
  85.1 19.1 %reduce = bf16[3584,256]{1,0:T(8,128)(2,1)S(1)} reduce(bf16[3584,1,256]{2,1,0:T(2,128)(2,1)} %bitcast.14, bf16[]{:T(256)} %broadcast.61), dimensions={1}, to_apply=%bitcast.11.reduce_sub_computation | reduce | bytes 3670018
  104.2 0.0 copy-start
  104.2 0.0 copy-start.1
  104.2 3.1 %reshape.79 = bf16[8,2,57344]{2,1,0:T(2,128)(2,1)} reshape(bf16[3584,256]{1,0:T(8,128)(2,1)S(1)} %reduce) | data formatting | bytes 3670016
  107.3 5.5 %all-to-all-start = ((bf16[8,2,57344]{2,1,0:T(2,128)(2,1)}), bf16[8,2,57344]{2,1,0:T(2,128)(2,1)S(1)}, u32[]{:S(2)}, u32[]{:S(2)}) async-start(bf16[8,2,57344]{2,1,0:T(2,128)(2,1)} %reshape.79), calls=%async_computation.1 | async-start | bytes 3670016 | tf_op jit(solution)/shard_map/all_to_all | solution.py:24
  112.9 0.1 copy.22
  112.9 0.1 reshape.60
  113.0 0.1 reshape.59
  113.2 42.2 %all-to-all-done = bf16[8,2,57344]{2,1,0:T(2,128)(2,1)S(1)} async-done(((bf16[8,2,57344]{2,1,0:T(2,128)(2,1)}), bf16[8,2,57344]{2,1,0:T(2,128)(2,1)S(1)}, u32[]{:S(2)}, u32[]{:S(2)}) %all-to-all-start) | async-done | bytes 1835040 | tf_op jit(solution)/shard_map/all_to_all | solution.py:24
  155.3 4.1 %reshape.80 = bf16[3584,1,256]{2,1,0:T(2,128)(2,1)} reshape(bf16[8,2,57344]{2,1,0:T(2,128)(2,1)S(1)} %all-to-all-done) | data formatting | bytes 3670016
  159.4 4.1 %copy.25 = f32[1,3584,256]{2,1,0:T(8,128)} copy(bf16[1,3584,256]{2,0,1:T(2,128)(2,1)} %bitcast.13) | data formatting | bytes 5505024
  163.5 4.7 %gather_fusion = f32[8,448,256]{2,1,0:T(8,128)} fusion(f32[8,448,256]{2,1,0:T(8,128)} %bitcast.12, s32[1024]{0:T(1024)S(1)} %pad_clamp_fusion.1), kind=kCustom, calls=%fused_computation | custom fusion | bytes 7340064 | tf_op jit(solution)/shard_map/jit(_take)/gather | solution.py:27
  168.2 9.6 %fusion.2 = (bf16[8,448,256]{2,1,0:T(8,128)(2,1)S(1)}, f32[8,448,256]{2,1,0:T(8,128)}, f32[8,448,256]{2,1,0:T(8,128)}, f32[8,448,256]{2,1,0:T(8,128)}) fusion(f32[8,448,256]{2,1,0:T(8,128)} %param.10, f32[8,448,256]{2,1,0:T(8,128)} %gather_fusion, pred[8]{0:T(512)(128)(4,1)S(1)} %compare_and_fusion.1, f32[8,448,256]{2,1,0:T(8,128)} %param.11, ...), kind=kLoop, calls=%fused_computation.16 | loop fusion | flops 15597568 | bytes 27525128 | tf_op jit(solution)/shard_map/convert_element_type | solution.py:35
  177.7 2.6 gather_fusion.1
  180.4 4.3 %broadcast_select_fusion = bf16[16,448,256]{2,1,0:T(8,128)(2,1)} fusion(bf16[16,448,256]{2,1,0:T(8,128)(2,1)} %gather_fusion.1, pred[16]{0:T(512)(128)(4,1)S(1)} %compare_and_fusion), kind=kLoop, calls=%fused_computation.7 | loop fusion | flops 1835008 | bytes 7340048 | tf_op jit(solution)/shard_map/jit(_take)/select_n | solution.py:36
  184.6 4.5 %all-to-all-start.1 = ((bf16[16,448,256]{2,1,0:T(8,128)(2,1)}), bf16[16,448,256]{2,1,0:T(8,128)(2,1)}, u32[]{:S(2)}, u32[]{:S(2)}) async-start(bf16[16,448,256]{2,1,0:T(8,128)(2,1)} %broadcast_select_fusion), calls=%async_computation.2 | async-start | bytes 7340032 | tf_op jit(solution)/shard_map/all_to_all | solution.py:37
  189.1 5.6 %multiply_add_fusion = f32[8,448,256]{2,1,0:T(8,128)} fusion(f32[8,448,256]{2,1,0:T(8,128)} %get-tuple-element.6, f32[8,448,256]{2,1,0:T(8,128)} %param.13), kind=kLoop, calls=%fused_computation.4 | loop fusion | flops 2752512 | bytes 11010048 | tf_op jit(solution)/shard_map/add | solution.py:34
  194.7 75.8 %all-to-all-done.1 = bf16[16,448,256]{2,1,0:T(8,128)(2,1)} async-done(((bf16[16,448,256]{2,1,0:T(8,128)(2,1)}), bf16[16,448,256]{2,1,0:T(8,128)(2,1)}, u32[]{:S(2)}, u32[]{:S(2)}) %all-to-all-start.1) | async-done | bytes 3670048 | tf_op jit(solution)/shard_map/all_to_all | solution.py:37
  270.5 4.2 %copy.24 = bf16[2,8,448,256]{3,2,1,0:T(8,128)(2,1)} copy(bf16[2,8,448,256]{3,2,0,1:T(8,128)(2,1)} %bitcast.3) | data formatting | bytes 7340032 | tf_op jit(solution)/shard_map/all_to_all | solution.py:37
  (8 shorter events, 0.0 us)
Async XLA Ops:
  7.2 70.7 %reduce-scatter.2.cloned.1.call-start = ((), (), s32[]{:S(2)}) async-start(), calls=%async_computation.3 | async-start | bytes 9175040 | tf_op jit(solution)/shard_map/reduce_scatter | solution.py:18
  104.2 8.6 %copy-start = (s32[8,2]{0,1:T(2,128)S(1)}, s32[8,2]{0,1:T(2,128)}, u32[]{:S(2)}) copy-start(s32[8,2]{0,1:T(2,128)} %param.9) | copy-start | bytes 196
  104.2 8.9 %copy-start.1 = (s32[8]{0:T(128)S(1)}, s32[8]{0:T(128)}, u32[]{:S(2)}) copy-start(s32[8]{0:T(128)} %param.8) | copy-start | bytes 100
  107.3 48.0 %all-to-all-start = ((bf16[8,2,57344]{2,1,0:T(2,128)(2,1)}), bf16[8,2,57344]{2,1,0:T(2,128)(2,1)S(1)}, u32[]{:S(2)}, u32[]{:S(2)}) async-start(bf16[8,2,57344]{2,1,0:T(2,128)(2,1)} %reshape.79), calls=%async_computation.1 | async-start | bytes 3670016 | tf_op jit(solution)/shard_map/all_to_all | solution.py:24
  184.6 85.9 %all-to-all-start.1 = ((bf16[16,448,256]{2,1,0:T(8,128)(2,1)}), bf16[16,448,256]{2,1,0:T(8,128)(2,1)}, u32[]{:S(2)}, u32[]{:S(2)}) async-start(bf16[16,448,256]{2,1,0:T(8,128)(2,1)} %broadcast_select_fusion), calls=%async_computation.2 | async-start | bytes 7340032 | tf_op jit(solution)/shard_map/all_to_all | solution.py:37
Sparse Core Ops, SparseCore 0:
  10.5 67.2 reduce-scatter.1
where the time goes:
time: 282 us
  waiting for transfers between devices  189 us (67%)
  other arithmetic  38.6 us (14%)
  local copies, waits for them, and re-layouts  30.3 us (11%)
  between operations  14.1 us (5%)
  starting transfers between devices  10 us (4%)
    all_to_all x1, waiting for transfers between devices, per_device(): lax.all_to_all(outgoing, 'expert', split_axis=0, concat_axis=1, tiled=True)  75.8 us
    reduce_scatter x1, waiting for transfers between devices, per_device(): lax.psum_scatter(grad_parts[0].astype(jnp.float32).astype(jnp.bfloat16),...  69.9 us
    all_to_all x1, waiting for transfers between devices, per_device(): lax.all_to_all(summed.astype(jnp.bfloat16), 'expert', split_axis=1, conca...  42.2 us
    unnamed x1, other arithmetic  19.1 us
    unnamed x9, local copies, waits for them, and re-layouts  11.9 us
    convert_element_type x1, other arithmetic, per_device(): updated_bf16 = master_out.astype(jnp.bfloat16)  9.56 us
    reduce_scatter x1, local copies, waits for them, and re-layouts, per_device(): lax.psum_scatter(grad_parts[0].astype(jnp.float32).astype(jnp.bfloat16),...  6.77 us
  transfers between devices with their start and end apart: 3, of which 3 were waited for; matrix products, arithmetic and copies ran while one was open for 2% of the time, Pallas kernels for 0%

commit v1 on v0

v1 whole, which is shorter than its diff:
```python
import functools

import jax
import jax.numpy as jnp
from jax import lax
from jax.experimental import pallas as pl
from jax.experimental.pallas import tpu as pltpu
from jax.sharding import PartitionSpec as P

STEP = 10


beta_one = 0.9
beta_two = 0.999
adam_eps = 1e-08
learn_rate = 0.05
decay_rate = 0.1
ema_decay = 0.99

MESH = pl.DeviceIdType.MESH
CORES = 2
VMEM_LIMIT = 60 * 1024 * 1024


def row_tile(rows, most):
    return max(t for t in range(16, most + 1, 16) if rows % t == 0)


def reduce_kernel(n_e, n_dp, grad, out, own, got, part, peer, done,
                  load_sem, pair_send, pair_recv, part_send, part_recv, out_send, out_recv, self_sem):
    chips = n_dp // CORES
    rows = grad.shape[0] // n_e
    cols = grad.shape[1] // n_dp
    e = lax.axis_index("expert")
    d = lax.axis_index("dp")
    chip, core = d // CORES, d % CORES
    other = 1 - core
    half = n_e // 2
    side, place = e // half, e % half

    barrier = pltpu.get_barrier_semaphore()
    for r in range(1, n_dp):
        pl.semaphore_signal(barrier, inc=1, device_id=(e, lax.rem(d + r, n_dp)), device_id_type=MESH)
    for r in range(1, n_e):
        pl.semaphore_signal(barrier, inc=1, device_id=(lax.rem(e + r, n_e), d), device_id_type=MESH)

    def holder(k):
        if k < half:
            return (1 - side) * half + lax.rem(place + k, half)
        return side * half + lax.rem(place + (k - half + 1), half)

    def block(k, chip_of, core_of):
        first = pl.multiple_of(holder(k) * rows, rows)
        column = pl.multiple_of((chip_of * CORES + core_of) * cols, cols)
        return grad.at[pl.ds(first, rows), pl.ds(column, cols)]

    def chip_at(r):
        return lax.rem(chip + 1 + r, chips)

    loads, pairs = {}, {}
    for k in range(n_e):
        for r in range(chips):
            loads[k, r] = pltpu.make_async_copy(block(k, chip_at(r), core), own.at[k, r], load_sem.at[k, r])
            loads[k, r].start()
    pl.semaphore_wait(barrier, n_dp - 1 + n_e - 1)
    for k in range(n_e):
        for r in range(chips):
            pairs[k, r] = pltpu.make_async_remote_copy(
                src_ref=block(k, chip_at(r), other), dst_ref=got.at[k, r],
                send_sem=pair_send.at[k, r], recv_sem=pair_recv.at[k, r],
                device_id=(e, chip * CORES + other), device_id_type=MESH)
            pairs[k, r].start()

    tile = row_tile(rows, 64)
    parts, outs = {}, {}

    def to_chips(k):
        for r in range(chips - 1):
            loads[k, r].wait()
            pairs[k, r].wait_recv()

            @pl.loop(0, rows // tile)
            def _(i):
                at = pl.ds(pl.multiple_of(i * tile, tile), tile)
                total = own[k, r, at, :].astype(jnp.float32) + got[k, r, at, :].astype(jnp.float32)
                part[k, r, at, :] = total.astype(jnp.bfloat16)

            parts[k, r] = pltpu.make_async_remote_copy(
                src_ref=part.at[k, r], dst_ref=peer.at[k, r],
                send_sem=part_send.at[k, r], recv_sem=part_recv.at[k, r],
                device_id=(e, chip_at(r) * CORES + core), device_id_type=MESH)
            parts[k, r].start()

    def to_holder(k):
        r_own = chips - 1
        loads[k, r_own].wait()
        pairs[k, r_own].wait_recv()
        for r in range(chips - 1):
            parts[k, r].wait_recv()

        @pl.loop(0, rows // tile)
        def _(i):
            at = pl.ds(pl.multiple_of(i * tile, tile), tile)
            total = own[k, r_own, at, :].astype(jnp.float32) + got[k, r_own, at, :].astype(jnp.float32)
            for r in range(chips - 1):
                total = total + peer[k, r, at, :].astype(jnp.float32)
            done[k, at, :] = total.astype(jnp.bfloat16)

        if k < n_e - 1:
            outs[k] = pltpu.make_async_remote_copy(
                src_ref=done.at[k], dst_ref=out.at[e],
                send_sem=out_send.at[k], recv_sem=out_recv.at[k],
                device_id=(holder(k), d), device_id_type=MESH)
        else:
            outs[k] = pltpu.make_async_copy(done.at[k], out.at[e], self_sem)
        outs[k].start()

    ahead = min(2, n_e)
    for k in range(ahead):
        to_chips(k)
    for k in range(n_e):
        if k + ahead < n_e:
            to_chips(k + ahead)
        to_holder(k)

    for k in range(n_e):
        for r in range(chips):
            pairs[k, r].wait_send()
        for r in range(chips - 1):
            parts[k, r].wait_send()
        outs[k].wait()


def owned_rows(n_e, n_dp, grad):
    rows, cols = grad.shape[0] // n_e, grad.shape[1] // n_dp
    chips = n_dp // CORES
    dma = pltpu.SemaphoreType.DMA
    sent = grad.size * 2
    return pl.pallas_call(
        functools.partial(reduce_kernel, n_e, n_dp),
        out_shape=jax.ShapeDtypeStruct((n_e, rows, cols), jnp.bfloat16),
        in_specs=[pl.BlockSpec(memory_space=pl.ANY)],
        out_specs=pl.BlockSpec(memory_space=pl.ANY),
        scratch_shapes=[
            pltpu.VMEM((n_e, chips, rows, cols), jnp.bfloat16),
            pltpu.VMEM((n_e, chips, rows, cols), jnp.bfloat16),
            pltpu.VMEM((n_e, chips - 1, rows, cols), jnp.bfloat16),
            pltpu.VMEM((n_e, chips - 1, rows, cols), jnp.bfloat16),
            pltpu.VMEM((n_e, rows, cols), jnp.bfloat16),
            dma((n_e, chips)),
            dma((n_e, chips)),
            dma((n_e, chips)),
            dma((n_e, chips - 1)),
            dma((n_e, chips - 1)),
            dma((n_e,)),
            dma((n_e,)),
            dma(()),
        ],
        compiler_params=pltpu.CompilerParams(
            collective_id=0, has_side_effects=True, vmem_limit_bytes=VMEM_LIMIT),
        cost_estimate=pl.CostEstimate(flops=2 * grad.size, bytes_accessed=2 * sent, transcendentals=0),
        name="reduce_rows",
    )(grad)


def adam(gradient, master, one, two):
    scale_one = 1.0 / (1.0 - beta_one**STEP)
    scale_two = 1.0 / (1.0 - beta_two**STEP)
    one_out = beta_one * one + (1.0 - beta_one) * gradient
    two_out = beta_two * two + (1.0 - beta_two) * gradient * gradient
    update = one_out * scale_one / (jnp.sqrt(two_out * scale_two) + adam_eps)
    return master - learn_rate * (update + decay_rate * master), one_out, two_out


def outgoing_kernel(owner, slots, rows_ref, master, one, two, out, held):
    n_e, tile, _ = master.shape
    step = row_tile(tile, 32)

    @pl.loop(0, n_e)
    def _(x):
        @pl.loop(0, tile // step)
        def _(i):
            at = pl.ds(pl.multiple_of(i * step, step), step)
            gradient = rows_ref[owner[x], at, :].astype(jnp.float32)
            held[x, at, :] = adam(gradient, master[x, at, :], one[x, at, :], two[x, at, :])[0].astype(jnp.bfloat16)

    @pl.loop(0, out.shape[0])
    def _(s):
        out[s] = held[slots[s]]


def outgoing_rows(owner_rows, owner_slot, slots, master, one, two):
    n_e, rows, cols = master.shape
    tile = row_tile(rows, 112)
    spec = pl.BlockSpec((n_e, tile, cols), lambda i, *_: (0, i, 0))
    return pl.pallas_call(
        outgoing_kernel,
        out_shape=jax.ShapeDtypeStruct((slots.shape[0], rows, cols), jnp.bfloat16),
        grid_spec=pltpu.PrefetchScalarGridSpec(
            num_scalar_prefetch=2, grid=(rows // tile,),
            in_specs=[spec] * 4,
            out_specs=pl.BlockSpec((slots.shape[0], tile, cols), lambda i, *_: (0, i, 0)),
            scratch_shapes=[pltpu.VMEM((n_e, tile, cols), jnp.bfloat16)]),
        compiler_params=pltpu.CompilerParams(vmem_limit_bytes=VMEM_LIMIT),
        cost_estimate=pl.CostEstimate(
            flops=16 * master.size, bytes_accessed=18 * master.size, transcendentals=2 * master.size),
        name="outgoing_rows",
    )(owner_slot, slots, owner_rows, master, one, two)


def update_kernel(owner, rows_ref, master, one, two, ema, master_out, one_out, two_out, ema_out):
    n_e, tile, _ = master.shape
    step = row_tile(tile, 32)

    @pl.loop(0, n_e)
    def _(x):
        @pl.loop(0, tile // step)
        def _(i):
            at = pl.ds(pl.multiple_of(i * step, step), step)
            gradient = rows_ref[owner[x], at, :].astype(jnp.float32)
            new, first, second = adam(gradient, master[x, at, :], one[x, at, :], two[x, at, :])
            master_out[x, at, :] = new
            one_out[x, at, :] = first
            two_out[x, at, :] = second
            ema_out[x, at, :] = ema_decay * ema[x, at, :] + (1.0 - ema_decay) * new


def updated_state(owner_rows, owner_slot, master, one, two, ema):
    n_e, rows, cols = master.shape
    tile = row_tile(rows, 112)
    spec = pl.BlockSpec((n_e, tile, cols), lambda i, *_: (0, i, 0))
    return pl.pallas_call(
        update_kernel,
        out_shape=[jax.ShapeDtypeStruct(master.shape, jnp.float32)] * 4,
        grid_spec=pltpu.PrefetchScalarGridSpec(
            num_scalar_prefetch=1, grid=(rows // tile,),
            in_specs=[spec] * 5, out_specs=[spec] * 4),
        compiler_params=pltpu.CompilerParams(vmem_limit_bytes=VMEM_LIMIT),
        cost_estimate=pl.CostEstimate(
            flops=20 * master.size, bytes_accessed=34 * master.size, transcendentals=2 * master.size),
        name="updated_state",
    )(owner_slot, owner_rows, master, one, two, ema)


def per_device(n_e, n_dp, grad_parts, owner_slot, slot_expert, master, moment_one, moment_two, ema_weights):
    owner_rows = owned_rows(n_e, n_dp, grad_parts[0, 0])
    outgoing = outgoing_rows(owner_rows, owner_slot, slot_expert.reshape(-1), master, moment_one, moment_two)
    replicas = lax.all_to_all(outgoing, "expert", split_axis=0, concat_axis=1, tiled=True)
    master_out, moment_one_out, moment_two_out, ema_out = updated_state(
        owner_rows, owner_slot, master, moment_one, moment_two, ema_weights)
    return (master_out, moment_one_out, moment_two_out, ema_out, replicas)


def solution(mesh):
    placed = (
        P("dp", "expert", None, None),
        P(),
        P(),
        P(None, "expert", "dp"),
        P(None, "expert", "dp"),
        P(None, "expert", "dp"),
        P(None, "expert", "dp"),
    )
    return jax.shard_map(
        functools.partial(per_device, mesh.shape["expert"], mesh.shape["dp"]),
        mesh=mesh,
        in_specs=placed,
        out_specs=(
            P(None, "expert", "dp"),
            P(None, "expert", "dp"),
            P(None, "expert", "dp"),
            P(None, "expert", "dp"),
            P("expert", None, "dp"),
        ),
        check_vma=False,
    )
```

time: 282 us -> 163 us (0.58)
  waiting for transfers between devices: 189 us -> 67.6 us
  Pallas kernels: 0 us -> 84 us
  other arithmetic: 38.6 us -> 0 us
  local copies, waits for them, and re-layouts: 30.3 us -> 5.55 us
  between operations: 14.1 us -> 0.65 us
  starting transfers between devices: 10 us -> 4.5 us
    pallas_call x0 -> x3, Pallas kernels: none -> 84 us  [the longest x1 57.8 us: owned_rows(): pl.pallas_call(functools.partial(reduce_kernel, n_e, n_dp), out_shape=jax...]
    reduce_scatter x1 -> x0, waiting for transfers between devices: 69.9 us -> none  [per_device(): lax.psum_scatter(grad_parts[0].astype(jnp.float32).astype(jnp.bfloat16),...]
    all_to_all x1 -> x0, waiting for transfers between devices: 42.2 us -> none  [per_device(): lax.all_to_all(summed.astype(jnp.bfloat16), 'expert', split_axis=1, conca...]
    unnamed x1 -> x0, other arithmetic: 19.1 us -> none
    unnamed x9 -> x1, local copies, waits for them, and re-layouts: 11.9 us -> 0.75 us
    convert_element_type x1 -> x0, other arithmetic: 9.56 us -> none  [per_device(): updated_bf16 = master_out.astype(jnp.bfloat16)]
    all_to_all x1, waiting for transfers between devices: 75.8 us -> 67.6 us  [per_device(): lax.all_to_all(outgoing, 'expert', split_axis=0, concat_axis=1, tiled=True)]
    gather x2 -> x0, local copies, waits for them, and re-layouts: 7.27 us -> none  [the longest x1 4.65 us: per_device(): gradient = jnp.take(owner_rows, owner_slot, axis=0)]
  transfers between devices with their start and end apart: 3 -> 1, of which waited for: 3 -> 1; matrix products, arithmetic and copies ran while one was open for 2% -> 0% of each run, Pallas kernels for 0% -> 9%
where the time goes in v1:
time: 163 us; the launch traced here: 162 us
  Pallas kernels  84 us (52%)
  waiting for transfers between devices  67.6 us (41%)
  local copies, waits for them, and re-layouts  5.55 us (3%)
  starting transfers between devices  4.5 us (3%)
    all_to_all x1, waiting for transfers between devices, per_device(): lax.all_to_all(outgoing, 'expert', split_axis=0, concat_axis=1, tiled=True)  67.6 us
    pallas_call x1, Pallas kernels, owned_rows(): pl.pallas_call(functools.partial(reduce_kernel, n_e, n_dp), out_shape=jax...  57.8 us
    pallas_call x1, Pallas kernels, updated_state(): pl.pallas_call(update_kernel, out_shape=[jax.ShapeDtypeStruct(master.shap...  14.9 us
    pallas_call x1, Pallas kernels, outgoing_rows(): pl.pallas_call(outgoing_kernel, out_shape=jax.ShapeDtypeStruct((slots.sha...  11.3 us
    all_to_all x1, starting transfers between devices, per_device(): lax.all_to_all(outgoing, 'expert', split_axis=0, concat_axis=1, tiled=True)  4.5 us
    all_to_all x1, local copies, waits for them, and re-layouts, per_device(): lax.all_to_all(outgoing, 'expert', split_axis=0, concat_axis=1, tiled=True)  4.2 us
  transfers between devices with their start and end apart: 1, of which 1 were waited for; matrix products, arithmetic and copies ran while one was open for 0% of the time, Pallas kernels for 9%

profile of v1, /device:TPU:0, one launch (start us, length us, event | category | flops | bytes accessed | tf_op | source)
XLA Modules:
  0.0 162.3 jit_solution(14309839970044960432)
XLA Ops:
  0.6 0.8 copy.14
  1.4 0.6 reshape.13.slots
  2.0 57.8 %reduce_rows.1.rows_ref = bf16[8,448,256]{2,1,0:T(8,128)(2,1)} custom-call(bf16[3584,1024]{1,0:T(8,128)(2,1)} %bitcast.5), custom_call_target="tpu_custom_call" | custom-call | flops 7340032 | bytes 14680064 | tf_op jit(solution)/shard_map/reduce_rows/pallas_call | solution.py:139
  59.8 11.3 %outgoing_rows.1 = bf16[16,448,256]{2,1,0:T(8,128)(2,1)} custom-call(s32[8]{0:T(128)} %owner.3, s32[16]{0:T(128)} %reshape.13.slots, bf16[8,448,256]{2,1,0:T(8,128)(2,1)} %reduce_rows.1.rows_ref, f32[8,448,256]{2,1,0:T(8,128)} %master.3, f32[8,448,256]{2,1,0:T(8,128)} %one.3, f32[8,448,256]{2,1,0:T(8,128)} %two.3), custom_call_target="tpu_custom_call" | custom-call | flops 14680064 | bytes 16515072 | tf_op jit(solution)/shard_map/outgoing_rows/pallas_call | solution.py:196
  71.1 4.5 %all-to-all-start = ((bf16[16,448,256]{2,1,0:T(8,128)(2,1)}), bf16[16,448,256]{2,1,0:T(8,128)(2,1)}, u32[]{:S(2)}, u32[]{:S(2)}) async-start(bf16[16,448,256]{2,1,0:T(8,128)(2,1)} %outgoing_rows.1), calls=%async_computation | async-start | bytes 7340032 | tf_op jit(solution)/shard_map/all_to_all | solution.py:248
  75.6 14.9 %updated_state.1 = (f32[8,448,256]{2,1,0:T(8,128)}, f32[8,448,256]{2,1,0:T(8,128)}, f32[8,448,256]{2,1,0:T(8,128)}, f32[8,448,256]{2,1,0:T(8,128)}) custom-call(s32[8]{0:T(128)} %owner.3, bf16[8,448,256]{2,1,0:T(8,128)(2,1)} %reduce_rows.1.rows_ref, f32[8,448,256]{2,1,0:T(8,128)} %master.3, f32[8,448,256]{2,1,0:T(8,128)} %one.3, f32[8,448,256]{2,1,0:T(8,128)} %two.3, ...), custom_call_target="tpu_custom_call" | custom-call | flops 18350080 | bytes 31195136 | tf_op jit(solution)/shard_map/updated_state/pallas_call | solution.py:232
  90.5 67.6 %all-to-all-done = bf16[16,448,256]{2,1,0:T(8,128)(2,1)} async-done(((bf16[16,448,256]{2,1,0:T(8,128)(2,1)}), bf16[16,448,256]{2,1,0:T(8,128)(2,1)}, u32[]{:S(2)}, u32[]{:S(2)}) %all-to-all-start) | async-done | bytes 3670048 | tf_op jit(solution)/shard_map/all_to_all | solution.py:248
  158.1 4.2 %copy.15 = bf16[2,8,448,256]{3,2,1,0:T(8,128)(2,1)} copy(bf16[2,8,448,256]{3,2,0,1:T(8,128)(2,1)} %bitcast.2) | data formatting | bytes 7340032 | tf_op jit(solution)/shard_map/all_to_all | solution.py:248
Async XLA Ops:
  71.1 87.0 %all-to-all-start = ((bf16[16,448,256]{2,1,0:T(8,128)(2,1)}), bf16[16,448,256]{2,1,0:T(8,128)(2,1)}, u32[]{:S(2)}, u32[]{:S(2)}) async-start(bf16[16,448,256]{2,1,0:T(8,128)(2,1)} %outgoing_rows.1), calls=%async_computation | async-start | bytes 7340032 | tf_op jit(solution)/shard_map/all_to_all | solution.py:248

commit v2 on v0

v2 whole, which is shorter than its diff:
```python
import functools

import jax
import jax.numpy as jnp
from jax import lax
from jax.experimental import pallas as pl
from jax.experimental.pallas import tpu as pltpu
from jax.sharding import PartitionSpec as P

STEP = 10


beta_one = 0.9
beta_two = 0.999
adam_eps = 1e-08
learn_rate = 0.05
decay_rate = 0.1
ema_decay = 0.99

MESH = pl.DeviceIdType.MESH
CORES = 2
VMEM_LIMIT = 60 * 1024 * 1024
CHUNKS = 2


def row_tile(rows, most):
    return max(t for t in range(16, most + 1, 16) if rows % t == 0)


def adam(gradient, master, one, two):
    scale_one = 1.0 / (1.0 - beta_one**STEP)
    scale_two = 1.0 / (1.0 - beta_two**STEP)
    one_out = beta_one * one + (1.0 - beta_one) * gradient
    two_out = beta_two * two + (1.0 - beta_two) * gradient * gradient
    update = one_out * scale_one / (jnp.sqrt(two_out * scale_two) + adam_eps)
    return master - learn_rate * (update + decay_rate * master), one_out, two_out


def exchange_kernel(n_e, n_dp, chunks, owner, slots, grad, master, one, two, replicas, rows_out, *refs):
    gathered, slotted = refs[:chunks], refs[chunks:2 * chunks]
    (own, got, part, peer, done, held, master_in, one_in, two_in,
     load_sem, pair_send, pair_recv, part_send, part_recv, out_send, out_recv,
     state_sem, rows_sem, slot_send, slot_recv, self_sem) = refs[2 * chunks:]
    chips = n_dp // CORES
    rows = grad.shape[0] // n_e
    cols = grad.shape[1] // n_dp
    size = rows // chunks
    e = lax.axis_index("expert")
    d = lax.axis_index("dp")
    chip, core = d // CORES, d % CORES
    other = 1 - core
    half = n_e // 2
    side, place = e // half, e % half
    tile = row_tile(size, 32)
    steps = chunks * n_e

    barrier = pltpu.get_barrier_semaphore()
    for r in range(1, n_dp):
        pl.semaphore_signal(barrier, inc=1, device_id=(e, lax.rem(d + r, n_dp)), device_id_type=MESH)
    for r in range(1, n_e):
        pl.semaphore_signal(barrier, inc=1, device_id=(lax.rem(e + r, n_e), d), device_id_type=MESH)

    def holder(k):
        if k < half:
            return (1 - side) * half + lax.rem(place + k, half)
        return side * half + lax.rem(place + (k - half + 1), half)

    def block(j, chip_of, core_of):
        first = pl.multiple_of(holder(j % n_e) * rows + (j // n_e) * size, size)
        column = pl.multiple_of((chip_of * CORES + core_of) * cols, cols)
        return grad.at[pl.ds(first, size), pl.ds(column, cols)]

    def chip_at(r):
        return lax.rem(chip + 1 + r, chips)

    loads, pairs = {}, {}
    for j in range(steps):
        for r in range(chips):
            loads[j, r] = pltpu.make_async_copy(block(j, chip_at(r), core), own.at[j, r], load_sem.at[j, r])
            loads[j, r].start()
    pl.semaphore_wait(barrier, n_dp - 1 + n_e - 1)
    for j in range(steps):
        for r in range(chips):
            pairs[j, r] = pltpu.make_async_remote_copy(
                src_ref=block(j, chip_at(r), other), dst_ref=got.at[j, r],
                send_sem=pair_send.at[j, r], recv_sem=pair_recv.at[j, r],
                device_id=(e, chip * CORES + other), device_id_type=MESH)
            pairs[j, r].start()
    states = [pltpu.make_async_copy(src, dst, state_sem.at[i]) for i, (src, dst) in
              enumerate(((master, master_in), (one, one_in), (two, two_in)))]
    for copy in states:
        copy.start()

    parts, outs, sends, kept = {}, {}, {}, {}

    def to_chips(j):
        for r in range(chips - 1):
            loads[j, r].wait()
            pairs[j, r].wait_recv()

            @pl.loop(0, size // tile)
            def _(i):
                at = pl.ds(pl.multiple_of(i * tile, tile), tile)
                total = own[j, r, at, :].astype(jnp.float32) + got[j, r, at, :].astype(jnp.float32)
                part[j, r, at, :] = total.astype(jnp.bfloat16)

            parts[j, r] = pltpu.make_async_remote_copy(
                src_ref=part.at[j, r], dst_ref=peer.at[j, r],
                send_sem=part_send.at[j, r], recv_sem=part_recv.at[j, r],
                device_id=(e, chip_at(r) * CORES + core), device_id_type=MESH)
            parts[j, r].start()

    def to_holder(j):
        c, k = j // n_e, j % n_e
        away = k < n_e - 1
        r_own = chips - 1
        loads[j, r_own].wait()
        pairs[j, r_own].wait_recv()
        for r in range(chips - 1):
            parts[j, r].wait_recv()

        @pl.loop(0, size // tile)
        def _(i):
            at = pl.ds(pl.multiple_of(i * tile, tile), tile)
            total = own[j, r_own, at, :].astype(jnp.float32) + got[j, r_own, at, :].astype(jnp.float32)
            for r in range(chips - 1):
                total = total + peer[j, r, at, :].astype(jnp.float32)
            if away:
                done[j, at, :] = total.astype(jnp.bfloat16)
            else:
                gathered[c][e, at, :] = total.astype(jnp.bfloat16)

        if away:
            outs[j] = pltpu.make_async_remote_copy(
                src_ref=done.at[j], dst_ref=gathered[c].at[e],
                send_sem=out_send.at[j], recv_sem=out_recv.at[j],
                device_id=(holder(k), d), device_id_type=MESH)
            outs[j].start()

    def to_hosts(c):
        for k in range(n_e - 1):
            outs[c * n_e + k].wait_recv()
        kept[c] = pltpu.make_async_copy(
            gathered[c], rows_out.at[:, pl.ds(c * size, size), :], rows_sem.at[c])
        kept[c].start()

        @pl.loop(0, n_e)
        def _(x):
            position = owner[x]

            @pl.loop(0, size // tile)
            def _(i):
                at = pl.ds(pl.multiple_of(i * tile, tile), tile)
                there = pl.ds(pl.multiple_of(c * size + i * tile, tile), tile)
                gradient = gathered[c][position, at, :].astype(jnp.float32)
                new = adam(gradient, master_in[x, there, :], one_in[x, there, :], two_in[x, there, :])[0]
                held[x, at, :] = new.astype(jnp.bfloat16)

        width = replicas.shape[0]
        for k in range(n_e):
            host = holder(k)
            for s in range(width):
                wanted = slots[host * width + s]

                @pl.loop(0, size // tile)
                def _(i):
                    at = pl.ds(pl.multiple_of(i * tile, tile), tile)
                    slotted[c][k, s, at, :] = held[wanted, at, :]

            first = pl.multiple_of(e * rows + c * size, size)
            target = replicas.at[:, pl.ds(first, size), :]
            j = c * n_e + k
            if k < n_e - 1:
                sends[j] = pltpu.make_async_remote_copy(
                    src_ref=slotted[c].at[k], dst_ref=target,
                    send_sem=slot_send.at[j], recv_sem=slot_recv.at[j],
                    device_id=(host, d), device_id_type=MESH)
            else:
                sends[j] = pltpu.make_async_copy(slotted[c].at[k], target, self_sem.at[c])
            sends[j].start()

    ahead = min(3, steps)
    for j in range(ahead):
        to_chips(j)
    for j in range(steps):
        if j + ahead < steps:
            to_chips(j + ahead)
        to_holder(j)

    for copy in states:
        copy.wait()
    for c in range(chunks):
        to_hosts(c)

    for j in range(steps):
        for r in range(chips):
            pairs[j, r].wait_send()
        for r in range(chips - 1):
            parts[j, r].wait_send()
        if j in outs:
            outs[j].wait_send()
    for c in range(chunks):
        kept[c].wait()
    for j in range(steps):
        sends[j].wait()


def exchanged(n_e, n_dp, grad, owner_slot, slot_expert, master, one, two):
    rows, cols = grad.shape[0] // n_e, grad.shape[1] // n_dp
    chips = n_dp // CORES
    width = slot_expert.shape[1]
    chunks = CHUNKS
    size = rows // chunks
    steps = chunks * n_e
    dma = pltpu.SemaphoreType.DMA
    half = jnp.bfloat16
    hbm = pl.BlockSpec(memory_space=pl.ANY)
    smem = pl.BlockSpec(memory_space=pltpu.SMEM)
    return pl.pallas_call(
        functools.partial(exchange_kernel, n_e, n_dp, chunks),
        out_shape=[
            jax.ShapeDtypeStruct((width, n_e * rows, cols), half),
            jax.ShapeDtypeStruct((n_e, rows, cols), half),
        ],
        in_specs=[smem, smem, hbm, hbm, hbm, hbm],
        out_specs=[hbm, hbm],
        scratch_shapes=[pltpu.VMEM((n_e, size, cols), half)] * chunks
        + [pltpu.VMEM((n_e, width, size, cols), half)] * chunks
        + [
            pltpu.VMEM((steps, chips, size, cols), half),
            pltpu.VMEM((steps, chips, size, cols), half),
            pltpu.VMEM((steps, chips - 1, size, cols), half),
            pltpu.VMEM((steps, chips - 1, size, cols), half),
            pltpu.VMEM((steps, size, cols), half),
            pltpu.VMEM((n_e, size, cols), half),
            pltpu.VMEM((n_e, rows, cols), jnp.float32),
            pltpu.VMEM((n_e, rows, cols), jnp.float32),
            pltpu.VMEM((n_e, rows, cols), jnp.float32),
            dma((steps, chips)),
            dma((steps, chips)),
            dma((steps, chips)),
            dma((steps, chips - 1)),
            dma((steps, chips - 1)),
            dma((steps,)),
            dma((steps,)),
            dma((3,)),
            dma((chunks,)),
            dma((steps,)),
            dma((steps,)),
            dma((chunks,)),
        ],
        compiler_params=pltpu.CompilerParams(
            collective_id=0, has_side_effects=True, vmem_limit_bytes=VMEM_LIMIT),
        name="exchange",
    )(owner_slot, slot_expert.reshape(-1), grad, master, one, two)


def update_kernel(owner, rows_ref, replicas, master, one, two, ema,
                  replicas_out, master_out, one_out, two_out, ema_out):
    n_e, tile, _ = master.shape
    step = row_tile(tile, 32)
    replicas_out[...] = replicas[...]

    @pl.loop(0, n_e)
    def _(x):
        @pl.loop(0, tile // step)
        def _(i):
            at = pl.ds(pl.multiple_of(i * step, step), step)
            gradient = rows_ref[owner[x], at, :].astype(jnp.float32)
            new, first, second = adam(gradient, master[x, at, :], one[x, at, :], two[x, at, :])
            master_out[x, at, :] = new
            one_out[x, at, :] = first
            two_out[x, at, :] = second
            ema_out[x, at, :] = ema_decay * ema[x, at, :] + (1.0 - ema_decay) * new


def updated_state(owner_rows, replicas, owner_slot, master, one, two, ema):
    n_e, rows, cols = master.shape
    tile = row_tile(rows, 64)
    spec = pl.BlockSpec((n_e, tile, cols), lambda i, *_: (0, i, 0))
    width, height, _ = replicas.shape
    slot_spec = pl.BlockSpec((width, height * tile // rows, cols), lambda i, *_: (0, i, 0))
    return pl.pallas_call(
        update_kernel,
        out_shape=[jax.ShapeDtypeStruct(replicas.shape, replicas.dtype)]
        + [jax.ShapeDtypeStruct(master.shape, jnp.float32)] * 4,
        grid_spec=pltpu.PrefetchScalarGridSpec(
            num_scalar_prefetch=1, grid=(rows // tile,),
            in_specs=[spec, slot_spec] + [spec] * 4, out_specs=[slot_spec] + [spec] * 4),
        compiler_params=pltpu.CompilerParams(vmem_limit_bytes=VMEM_LIMIT),
        name="updated_state",
    )(owner_slot, owner_rows, replicas, master, one, two, ema)


def per_device(n_e, n_dp, grad_parts, owner_slot, slot_expert, master, moment_one, moment_two, ema_weights):
    arrived, owner_rows = exchanged(
        n_e, n_dp, grad_parts[0, 0], owner_slot, slot_expert, master, moment_one, moment_two)
    replicas, master_out, moment_one_out, moment_two_out, ema_out = updated_state(
        owner_rows, arrived, owner_slot, master, moment_one, moment_two, ema_weights)
    return (master_out, moment_one_out, moment_two_out, ema_out, replicas)


def solution(mesh):
    placed = (
        P("dp", "expert", None, None),
        P(),
        P(),
        P(None, "expert", "dp"),
        P(None, "expert", "dp"),
        P(None, "expert", "dp"),
        P(None, "expert", "dp"),
    )
    return jax.shard_map(
        functools.partial(per_device, mesh.shape["expert"], mesh.shape["dp"]),
        mesh=mesh,
        in_specs=placed,
        out_specs=(
            P(None, "expert", "dp"),
            P(None, "expert", "dp"),
            P(None, "expert", "dp"),
            P(None, "expert", "dp"),
            P("expert", None, "dp"),
        ),
        check_vma=False,
    )
```

time: 282 us -> 157 us (0.56)
  waiting for transfers between devices: 189 us -> 0 us
  Pallas kernels: 0 us -> 154 us
  other arithmetic: 38.6 us -> 0 us
  local copies, waits for them, and re-layouts: 30.3 us -> 1.35 us
  between operations: 14.1 us -> 0.64 us
  starting transfers between devices: 10 us -> 0 us
    pallas_call x0 -> x2, Pallas kernels: none -> 154 us  [the longest x1 136 us: exchanged(): pl.pallas_call(functools.partial(exchange_kernel, n_e, n_dp, chunks), out...]
    all_to_all x2 -> x0, waiting for transfers between devices: 118 us -> none  [the longest x1 75.8 us: per_device(): lax.all_to_all(outgoing, 'expert', split_axis=0, concat_axis=1, tiled=True)]
    reduce_scatter x1 -> x0, waiting for transfers between devices: 69.9 us -> none  [per_device(): lax.psum_scatter(grad_parts[0].astype(jnp.float32).astype(jnp.bfloat16),...]
    unnamed x1 -> x0, other arithmetic: 19.1 us -> none
    unnamed x9 -> x1, local copies, waits for them, and re-layouts: 11.9 us -> 0.75 us
    all_to_all x2 -> x0, starting transfers between devices: 10 us -> none  [the longest x1 5.52 us: per_device(): lax.all_to_all(summed.astype(jnp.bfloat16), 'expert', split_axis=1, conca...]
    convert_element_type x1 -> x0, other arithmetic: 9.56 us -> none  [per_device(): updated_bf16 = master_out.astype(jnp.bfloat16)]
    gather x2 -> x0, local copies, waits for them, and re-layouts: 7.27 us -> none  [the longest x1 4.65 us: per_device(): gradient = jnp.take(owner_rows, owner_slot, axis=0)]
  transfers between devices with their start and end apart: 3 -> 0, of which waited for: 3 -> 0; matrix products, arithmetic and copies ran while one was open for 2% -> 0% of each run, Pallas kernels for 0% -> 0%
where the time goes in v2:
time: 157 us; the launch traced here: 156 us
  Pallas kernels  154 us (98%)
    pallas_call x1, Pallas kernels, exchanged(): pl.pallas_call(functools.partial(exchange_kernel, n_e, n_dp, chunks), out...  136 us
    pallas_call x1, Pallas kernels, updated_state(): pl.pallas_call(update_kernel, out_shape=[jax.ShapeDtypeStruct(replicas.sh...  18 us

profile of v2, /device:TPU:0, one launch (start us, length us, event | category | flops | bytes accessed | tf_op | source)
XLA Modules:
  0.0 155.8 jit_solution(5134125717572751640)
XLA Ops:
  0.6 0.8 copy.13
  1.4 0.6 reshape.13.slots
  2.0 135.8 %exchange.1 = (bf16[2,3584,256]{2,1,0:T(8,128)(2,1)}, bf16[8,448,256]{2,1,0:T(8,128)(2,1)}) custom-call(s32[8]{0:T(128)} %owner.3, s32[16]{0:T(128)} %reshape.13.slots, bf16[3584,1024]{1,0:T(8,128)(2,1)} %bitcast.1, f32[8,448,256]{2,1,0:T(8,128)} %master.3, f32[8,448,256]{2,1,0:T(8,128)} %one.3, f32[8,448,256]{2,1,0:T(8,128)} %two.3), custom_call_target="tpu_custom_call" | custom-call | tf_op jit(solution)/shard_map/exchange/pallas_call | solution.py:219
  137.8 18.0 %updated_state.1 = (bf16[2,3584,256]{2,1,0:T(8,128)(2,1)}, f32[8,448,256]{2,1,0:T(8,128)}, f32[8,448,256]{2,1,0:T(8,128)}, f32[8,448,256]{2,1,0:T(8,128)}, f32[8,448,256]{2,1,0:T(8,128)}) custom-call(s32[8]{0:T(128)} %owner.3, bf16[8,448,256]{2,1,0:T(8,128)(2,1)} %get-tuple-element.12.rows_ref, bf16[2,3584,256]{2,1,0:T(8,128)(2,1)} %get-tuple-element.13.replicas, ...), custom_call_target="tpu_custom_call" | custom-call | tf_op jit(solution)/shard_map/updated_state/pallas_call | solution.py:283

commit v3 on v2

--- a/solution.py
+++ b/solution.py
@@ -19,7 +19,7 @@
 
 MESH = pl.DeviceIdType.MESH
 CORES = 2
-VMEM_LIMIT = 60 * 1024 * 1024
+VMEM_LIMIT = 40 * 1024 * 1024
 CHUNKS = 2
 
 
@@ -36,11 +36,12 @@
     return master - learn_rate * (update + decay_rate * master), one_out, two_out
 
 
-def exchange_kernel(n_e, n_dp, chunks, owner, slots, grad, master, one, two, replicas, rows_out, *refs):
+def exchange_kernel(n_e, n_dp, chunks, owner, slots, grad, master, one, two, ema,
+                    master_out, one_out, two_out, ema_out, replicas, *refs):
     gathered, slotted = refs[:chunks], refs[chunks:2 * chunks]
-    (own, got, part, peer, done, held, master_in, one_in, two_in,
+    (own, got, part, peer, done, held,
      load_sem, pair_send, pair_recv, part_send, part_recv, out_send, out_recv,
-     state_sem, rows_sem, slot_send, slot_recv, self_sem) = refs[2 * chunks:]
+     state_sem, slot_send, slot_recv, self_sem) = refs[2 * chunks:]
     chips = n_dp // CORES
     rows = grad.shape[0] // n_e
     cols = grad.shape[1] // n_dp
@@ -87,11 +88,11 @@
                 device_id=(e, chip * CORES + other), device_id_type=MESH)
             pairs[j, r].start()
     states = [pltpu.make_async_copy(src, dst, state_sem.at[i]) for i, (src, dst) in
-              enumerate(((master, master_in), (one, one_in), (two, two_in)))]
+              enumerate(((master, master_out), (one, one_out), (two, two_out), (ema, ema_out)))]
     for copy in states:
         copy.start()
 
-    parts, outs, sends, kept = {}, {}, {}, {}
+    parts, outs, sends = {}, {}, {}
 
     def to_chips(j):
         for r in range(chips - 1):
@@ -140,9 +141,6 @@
     def to_hosts(c):
         for k in range(n_e - 1):
             outs[c * n_e + k].wait_recv()
-        kept[c] = pltpu.make_async_copy(
-            gathered[c], rows_out.at[:, pl.ds(c * size, size), :], rows_sem.at[c])
-        kept[c].start()
 
         @pl.loop(0, n_e)
         def _(x):
@@ -153,8 +151,12 @@
                 at = pl.ds(pl.multiple_of(i * tile, tile), tile)
                 there = pl.ds(pl.multiple_of(c * size + i * tile, tile), tile)
                 gradient = gathered[c][position, at, :].astype(jnp.float32)
-                new = adam(gradient, master_in[x, there, :], one_in[x, there, :], two_in[x, there, :])[0]
+                new, first, second = adam(
+                    gradient, master_out[x, there, :], one_out[x, there, :], two_out[x, there, :])
                 held[x, at, :] = new.astype(jnp.bfloat16)
+                master_out[x, there, :] = new
+                one_out[x, there, :] = first
+                two_out[x, there, :] = second
 
         width = replicas.shape[0]
         for k in range(n_e):
@@ -179,6 +181,14 @@
                 sends[j] = pltpu.make_async_copy(slotted[c].at[k], target, self_sem.at[c])
             sends[j].start()
 
+        @pl.loop(0, n_e)
+        def _(x):
+            @pl.loop(0, size // tile)
+            def _(i):
+                there = pl.ds(pl.multiple_of(c * size + i * tile, tile), tile)
+                ema_out[x, there, :] = (
+                    ema_decay * ema_out[x, there, :] + (1.0 - ema_decay) * master_out[x, there, :])
+
     ahead = min(3, steps)
     for j in range(ahead):
         to_chips(j)
@@ -199,13 +209,11 @@
             parts[j, r].wait_send()
         if j in outs:
             outs[j].wait_send()
-    for c in range(chunks):
-        kept[c].wait()
     for j in range(steps):
         sends[j].wait()
 
 
-def exchanged(n_e, n_dp, grad, owner_slot, slot_expert, master, one, two):
+def exchanged(n_e, n_dp, grad, owner_slot, slot_expert, master, one, two, ema):
     rows, cols = grad.shape[0] // n_e, grad.shape[1] // n_dp
     chips = n_dp // CORES
     width = slot_expert.shape[1]
@@ -215,15 +223,13 @@
     dma = pltpu.SemaphoreType.DMA
     half = jnp.bfloat16
     hbm = pl.BlockSpec(memory_space=pl.ANY)
+    vmem = pl.BlockSpec(memory_space=pltpu.VMEM)
     smem = pl.BlockSpec(memory_space=pltpu.SMEM)
     return pl.pallas_call(
         functools.partial(exchange_kernel, n_e, n_dp, chunks),
-        out_shape=[
-            jax.ShapeDtypeStruct((width, n_e * rows, cols), half),
-            jax.ShapeDtypeStruct((n_e, rows, cols), half),
-        ],
-        in_specs=[smem, smem, hbm, hbm, hbm, hbm],
-        out_specs=[hbm, hbm],
+        out_shape=[pltpu.VMEM(master.shape, jnp.float32)] * 4 + [pltpu.VMEM((width, n_e * rows, cols), half)],
+        in_specs=[smem, smem] + [hbm] * 5,
+        out_specs=[vmem] * 5,
         scratch_shapes=[pltpu.VMEM((n_e, size, cols), half)] * chunks
         + [pltpu.VMEM((n_e, width, size, cols), half)] * chunks
         + [
@@ -233,9 +239,6 @@
             pltpu.VMEM((steps, chips - 1, size, cols), half),
             pltpu.VMEM((steps, size, cols), half),
             pltpu.VMEM((n_e, size, cols), half),
-            pltpu.VMEM((n_e, rows, cols), jnp.float32),
-            pltpu.VMEM((n_e, rows, cols), jnp.float32),
-            pltpu.VMEM((n_e, rows, cols), jnp.float32),
             dma((steps, chips)),
             dma((steps, chips)),
             dma((steps, chips)),
@@ -243,8 +246,7 @@
             dma((steps, chips - 1)),
             dma((steps,)),
             dma((steps,)),
-            dma((3,)),
-            dma((chunks,)),
+            dma((4,)),
             dma((steps,)),
             dma((steps,)),
             dma((chunks,)),
@@ -252,52 +254,12 @@
         compiler_params=pltpu.CompilerParams(
             collective_id=0, has_side_effects=True, vmem_limit_bytes=VMEM_LIMIT),
         name="exchange",
-    )(owner_slot, slot_expert.reshape(-1), grad, master, one, two)
-
-
-def update_kernel(owner, rows_ref, replicas, master, one, two, ema,
-                  replicas_out, master_out, one_out, two_out, ema_out):
-    n_e, tile, _ = master.shape
-    step = row_tile(tile, 32)
-    replicas_out[...] = replicas[...]
-
-    @pl.loop(0, n_e)
-    def _(x):
-        @pl.loop(0, tile // step)
-        def _(i):
-            at = pl.ds(pl.multiple_of(i * step, step), step)
-            gradient = rows_ref[owner[x], at, :].astype(jnp.float32)
-            new, first, second = adam(gradient, master[x, at, :], one[x, at, :], two[x, at, :])
-            master_out[x, at, :] = new
-            one_out[x, at, :] = first
-            two_out[x, at, :] = second
-            ema_out[x, at, :] = ema_decay * ema[x, at, :] + (1.0 - ema_decay) * new
-
-
-def updated_state(owner_rows, replicas, owner_slot, master, one, two, ema):
-    n_e, rows, cols = master.shape
-    tile = row_tile(rows, 64)
-    spec = pl.BlockSpec((n_e, tile, cols), lambda i, *_: (0, i, 0))
-    width, height, _ = replicas.shape
-    slot_spec = pl.BlockSpec((width, height * tile // rows, cols), lambda i, *_: (0, i, 0))
-    return pl.pallas_call(
-        update_kernel,
-        out_shape=[jax.ShapeDtypeStruct(replicas.shape, replicas.dtype)]
-        + [jax.ShapeDtypeStruct(master.shape, jnp.float32)] * 4,
-        grid_spec=pltpu.PrefetchScalarGridSpec(
-            num_scalar_prefetch=1, grid=(rows // tile,),
-            in_specs=[spec, slot_spec] + [spec] * 4, out_specs=[slot_spec] + [spec] * 4),
-        compiler_params=pltpu.CompilerParams(vmem_limit_bytes=VMEM_LIMIT),
-        name="updated_state",
-    )(owner_slot, owner_rows, replicas, master, one, two, ema)
+    )(owner_slot, slot_expert.reshape(-1), grad, master, one, two, ema)
 
 
 def per_device(n_e, n_dp, grad_parts, owner_slot, slot_expert, master, moment_one, moment_two, ema_weights):
-    arrived, owner_rows = exchanged(
-        n_e, n_dp, grad_parts[0, 0], owner_slot, slot_expert, master, moment_one, moment_two)
-    replicas, master_out, moment_one_out, moment_two_out, ema_out = updated_state(
-        owner_rows, arrived, owner_slot, master, moment_one, moment_two, ema_weights)
-    return (master_out, moment_one_out, moment_two_out, ema_out, replicas)
+    return tuple(exchanged(
+        n_e, n_dp, grad_parts[0, 0], owner_slot, slot_expert, master, moment_one, moment_two, ema_weights))
 
 
 def solution(mesh):

time: 157 us -> 148 us (0.943)
  Pallas kernels: 154 us -> 136 us
  local copies, waits for them, and re-layouts: 1.35 us -> 10.5 us
    pallas_call x1 -> x0, Pallas kernels: 18 us -> none  [updated_state(): pl.pallas_call(update_kernel, out_shape=[jax.ShapeDtypeStruct(replicas.sh...]
    unnamed x1 -> x6, local copies, waits for them, and re-layouts: 0.75 us -> 9.94 us
where the time goes in v3:
time: 148 us; the launch traced here: 147 us
  Pallas kernels  136 us (92%)
  local copies, waits for them, and re-layouts  10.5 us (7%)
    pallas_call x1, Pallas kernels, exchanged(): pl.pallas_call(functools.partial(exchange_kernel, n_e, n_dp, chunks), out...  136 us
    unnamed x6, local copies, waits for them, and re-layouts  9.94 us

profile of v3, /device:TPU:0, one launch (start us, length us, event | category | flops | bytes accessed | tf_op | source)
XLA Modules:
  0.0 146.9 jit_solution(9617976449247111415)
XLA Ops:
  0.6 0.8 copy.13
  1.4 0.6 reshape.13.slots
  2.0 135.8 %exchange.1 = (f32[8,448,256]{2,1,0:T(8,128)S(1)}, f32[8,448,256]{2,1,0:T(8,128)S(1)}, f32[8,448,256]{2,1,0:T(8,128)S(1)}, f32[8,448,256]{2,1,0:T(8,128)S(1)}, bf16[2,3584,256]{2,1,0:T(8,128)(2,1)S(1)}) custom-call(s32[8]{0:T(128)} %owner.1, s32[16]{0:T(128)} %reshape.13.slots, bf16[3584,1024]{1,0:T(8,128)(2,1)} %bitcast.1, f32[8,448,256]{2,1,0:T(8,128)} %master.1, ...), custom_call_target="tpu_custom_call" | custom-call | tf_op jit(solution)/shard_map/exchange/pallas_call | solution.py:228
  137.8 1.8 %copy.19 = f32[8,448,256]{2,1,0:T(8,128)} copy(f32[8,448,256]{2,1,0:T(8,128)S(1)} %get-tuple-element.5) | data formatting | bytes 7340032
  139.6 1.8 %copy.20 = f32[8,448,256]{2,1,0:T(8,128)} copy(f32[8,448,256]{2,1,0:T(8,128)S(1)} %get-tuple-element.6) | data formatting | bytes 7340032
  141.4 1.8 %copy.21 = f32[8,448,256]{2,1,0:T(8,128)} copy(f32[8,448,256]{2,1,0:T(8,128)S(1)} %get-tuple-element.7) | data formatting | bytes 7340032
  143.3 1.8 %copy.22 = f32[8,448,256]{2,1,0:T(8,128)} copy(f32[8,448,256]{2,1,0:T(8,128)S(1)} %get-tuple-element.8) | data formatting | bytes 7340032
  145.1 1.8 %copy.23 = bf16[2,3584,256]{2,1,0:T(8,128)(2,1)} copy(bf16[2,3584,256]{2,1,0:T(8,128)(2,1)S(1)} %get-tuple-element.9) | data formatting | bytes 7340032

commit v4 on v3

--- a/solution.py
+++ b/solution.py
@@ -138,7 +138,7 @@
                 device_id=(holder(k), d), device_id_type=MESH)
             outs[j].start()
 
-    def to_hosts(c):
+    def update(c):
         for k in range(n_e - 1):
             outs[c * n_e + k].wait_recv()
 
@@ -169,18 +169,20 @@
                     at = pl.ds(pl.multiple_of(i * tile, tile), tile)
                     slotted[c][k, s, at, :] = held[wanted, at, :]
 
-            first = pl.multiple_of(e * rows + c * size, size)
-            target = replicas.at[:, pl.ds(first, size), :]
-            j = c * n_e + k
-            if k < n_e - 1:
-                sends[j] = pltpu.make_async_remote_copy(
-                    src_ref=slotted[c].at[k], dst_ref=target,
-                    send_sem=slot_send.at[j], recv_sem=slot_recv.at[j],
-                    device_id=(host, d), device_id_type=MESH)
-            else:
-                sends[j] = pltpu.make_async_copy(slotted[c].at[k], target, self_sem.at[c])
-            sends[j].start()
-
+    def to_host(j):
+        c, k = j // n_e, j % n_e
+        first = pl.multiple_of(e * rows + c * size, size)
+        target = replicas.at[:, pl.ds(first, size), :]
+        if k < n_e - 1:
+            sends[j] = pltpu.make_async_remote_copy(
+                src_ref=slotted[c].at[k], dst_ref=target,
+                send_sem=slot_send.at[j], recv_sem=slot_recv.at[j],
+                device_id=(holder(k), d), device_id_type=MESH)
+        else:
+            sends[j] = pltpu.make_async_copy(slotted[c].at[k], target, self_sem.at[c])
+        sends[j].start()
+
+    def average(c):
         @pl.loop(0, n_e)
         def _(x):
             @pl.loop(0, size // tile)
@@ -192,15 +194,27 @@
     ahead = min(3, steps)
     for j in range(ahead):
         to_chips(j)
-    for j in range(steps):
-        if j + ahead < steps:
-            to_chips(j + ahead)
-        to_holder(j)
-
-    for copy in states:
-        copy.wait()
     for c in range(chunks):
-        to_hosts(c)
+        last = c == chunks - 1
+        if c == 0:
+            for j in range(n_e):
+                to_chips(j + ahead) if j + ahead < steps else None
+                to_holder(j)
+        if not last:
+            for j in range((c + 1) * n_e, (c + 1) * n_e + half):
+                to_chips(j + ahead) if j + ahead < steps else None
+                to_holder(j)
+            for j in range((c + 1) * n_e + half + ahead, min((c + 2) * n_e + ahead, steps)):
+                to_chips(j)
+        if c == 0:
+            for copy in states:
+                copy.wait()
+        update(c)
+        for k in range(n_e):
+            to_host(c * n_e + k)
+            if not last and k < half:
+                to_holder((c + 1) * n_e + half + k)
+        average(c)
 
     for j in range(steps):
         for r in range(chips):

time: 148 us -> 149 us (level)
  Pallas kernels: 136 us -> 138 us
    pallas_call x1, Pallas kernels: 136 us -> 138 us  [exchanged(): pl.pallas_call(functools.partial(exchange_kernel, n_e, n_dp, chunks), out...]
where the time goes in v4:
time: 149 us
  Pallas kernels  138 us (93%)
  local copies, waits for them, and re-layouts  10.5 us (7%)
    pallas_call x1, Pallas kernels, exchanged(): pl.pallas_call(functools.partial(exchange_kernel, n_e, n_dp, chunks), out...  138 us
    unnamed x6, local copies, waits for them, and re-layouts  9.94 us

profile of v4, /device:TPU:0, one launch (start us, length us, event | category | flops | bytes accessed | tf_op | source)
XLA Modules:
  0.0 149.1 jit_solution(11266993217795778741)
XLA Ops:
  0.6 0.8 copy.13
  1.4 0.6 reshape.13.slots
  2.0 138.0 %exchange.1 = (f32[8,448,256]{2,1,0:T(8,128)S(1)}, f32[8,448,256]{2,1,0:T(8,128)S(1)}, f32[8,448,256]{2,1,0:T(8,128)S(1)}, f32[8,448,256]{2,1,0:T(8,128)S(1)}, bf16[2,3584,256]{2,1,0:T(8,128)(2,1)S(1)}) custom-call(s32[8]{0:T(128)} %owner.1, s32[16]{0:T(128)} %reshape.13.slots, bf16[3584,1024]{1,0:T(8,128)(2,1)} %bitcast.1, f32[8,448,256]{2,1,0:T(8,128)} %master.1, ...), custom_call_target="tpu_custom_call" | custom-call | tf_op jit(solution)/shard_map/exchange/pallas_call | solution.py:242
  139.9 1.8 %copy.19 = f32[8,448,256]{2,1,0:T(8,128)} copy(f32[8,448,256]{2,1,0:T(8,128)S(1)} %get-tuple-element.5) | data formatting | bytes 7340032
  141.8 1.8 %copy.20 = f32[8,448,256]{2,1,0:T(8,128)} copy(f32[8,448,256]{2,1,0:T(8,128)S(1)} %get-tuple-element.6) | data formatting | bytes 7340032
  143.6 1.8 %copy.21 = f32[8,448,256]{2,1,0:T(8,128)} copy(f32[8,448,256]{2,1,0:T(8,128)S(1)} %get-tuple-element.7) | data formatting | bytes 7340032
  145.5 1.8 %copy.22 = f32[8,448,256]{2,1,0:T(8,128)} copy(f32[8,448,256]{2,1,0:T(8,128)S(1)} %get-tuple-element.8) | data formatting | bytes 7340032
  147.3 1.8 %copy.23 = bf16[2,3584,256]{2,1,0:T(8,128)(2,1)} copy(bf16[2,3584,256]{2,1,0:T(8,128)(2,1)S(1)} %get-tuple-element.9) | data formatting | bytes 7340032

commit v5 on v3

--- a/solution.py
+++ b/solution.py
@@ -62,9 +62,11 @@
         pl.semaphore_signal(barrier, inc=1, device_id=(lax.rem(e + r, n_e), d), device_id_type=MESH)
 
     def holder(k):
-        if k < half:
-            return (1 - side) * half + lax.rem(place + k, half)
-        return side * half + lax.rem(place + (k - half + 1), half)
+        if k == n_e - 1:
+            return e
+        if k % 2 == 0:
+            return (1 - side) * half + lax.rem(place + k // 2, half)
+        return side * half + lax.rem(place + k // 2 + 1, half)
 
     def block(j, chip_of, core_of):
         first = pl.multiple_of(holder(j % n_e) * rows + (j // n_e) * size, size)

time: 148 us -> 147 us (level)
  Pallas kernels: 136 us -> 134 us
where the time goes in v5:
time: 147 us; the launch traced here: 146 us
  Pallas kernels  134 us (91%)
  local copies, waits for them, and re-layouts  10.5 us (7%)
    pallas_call x1, Pallas kernels, exchanged(): pl.pallas_call(functools.partial(exchange_kernel, n_e, n_dp, chunks), out...  134 us
    unnamed x6, local copies, waits for them, and re-layouts  9.94 us

profile of v5, /device:TPU:0, one launch (start us, length us, event | category | flops | bytes accessed | tf_op | source)
XLA Modules:
  0.0 145.5 jit_solution(8613771347906046262)
XLA Ops:
  0.6 0.8 copy.13
  1.4 0.6 reshape.13.slots
  2.0 134.3 %exchange.1 = (f32[8,448,256]{2,1,0:T(8,128)S(1)}, f32[8,448,256]{2,1,0:T(8,128)S(1)}, f32[8,448,256]{2,1,0:T(8,128)S(1)}, f32[8,448,256]{2,1,0:T(8,128)S(1)}, bf16[2,3584,256]{2,1,0:T(8,128)(2,1)S(1)}) custom-call(s32[8]{0:T(128)} %owner.1, s32[16]{0:T(128)} %reshape.13.slots, bf16[3584,1024]{1,0:T(8,128)(2,1)} %bitcast.1, f32[8,448,256]{2,1,0:T(8,128)} %master.1, ...), custom_call_target="tpu_custom_call" | custom-call | tf_op jit(solution)/shard_map/exchange/pallas_call | solution.py:230
  136.3 1.8 %copy.19 = f32[8,448,256]{2,1,0:T(8,128)} copy(f32[8,448,256]{2,1,0:T(8,128)S(1)} %get-tuple-element.5) | data formatting | bytes 7340032
  138.2 1.8 %copy.20 = f32[8,448,256]{2,1,0:T(8,128)} copy(f32[8,448,256]{2,1,0:T(8,128)S(1)} %get-tuple-element.6) | data formatting | bytes 7340032
  140.0 1.8 %copy.21 = f32[8,448,256]{2,1,0:T(8,128)} copy(f32[8,448,256]{2,1,0:T(8,128)S(1)} %get-tuple-element.7) | data formatting | bytes 7340032
  141.8 1.8 %copy.22 = f32[8,448,256]{2,1,0:T(8,128)} copy(f32[8,448,256]{2,1,0:T(8,128)S(1)} %get-tuple-element.8) | data formatting | bytes 7340032
  143.7 1.8 %copy.23 = bf16[2,3584,256]{2,1,0:T(8,128)(2,1)} copy(bf16[2,3584,256]{2,1,0:T(8,128)(2,1)S(1)} %get-tuple-element.9) | data formatting | bytes 7340032
